TPU v7x, 256 devices: a whole 4x4x8 slice. The times are simulated.
256 devices in a mesh: ctx: 32 (over x_lo, z, core), exp: 8 (over x_hi, y).
Axes of the slice: x: 4 (x_hi: 2, x_lo: 2; x = x_hi * 2 + x_lo), y: 4, z: 8, core: 2. Of those that a mesh axis runs over, the one named last changes fastest.
Arguments:
- queries: bfloat16 [8192, 8192], P('ctx', 'exp'), may hold values from -8 to 8
- keys: bfloat16 [8192, 512], P('ctx'), may hold values from -4 to 4
- values: bfloat16 [8192, 512], P('ctx'), may hold values from -6 to 6
- w_out: bfloat16 [8192, 4096], P('exp'), may hold values from -0.5 to 0.5
- residual: bfloat16 [8192, 4096], P(('ctx', 'exp')), may hold values from -1.5 to 1.5
- norm_gain: bfloat16 [4096], replicated, may hold values from 0.099609375 to 1.8984375
- expert_ids: int32 [8192, 2], P(('ctx', 'exp')), may hold values from 0 to 7, all different within a row; in each aligned block of 32 rows (0 to 31, 32 to 63, ...) at most 16 rows name the same one
- gate_weights: float32 [8192, 2], P(('ctx', 'exp')), may hold values from 0.2 to 1
- w_gate: bfloat16 [8, 4096, 768], P('exp', 'ctx'), may hold values from -0.09375 to 0.09375
- w_up: bfloat16 [8, 4096, 768], P('exp', 'ctx'), may hold values from -0.09375 to 0.09375
- w_down: bfloat16 [8, 768, 4096], P('exp', None, 'ctx'), may hold values from -0.21875 to 0.21875
Outputs:
- layer_out: bfloat16 [8192, 4096], P(('ctx', 'exp'))
Inputs may be any that keep to these rules, and one draw needn't show every extreme that they name: `expert_ids`: each row names 2 different experts; within each aligned block of 32 rows (the rows of one device) no expert is named by more than 16 rows.
All inputs are finite; a program needn't handle non-finite values.
Results may differ from a plain program's by a relative error of at most 0.025.
Values may be sent and summed in bfloat16 or wider, within the bound.
A program may use at most 128 MiB of HBM per device.

v0:
```python
import math
import jax
import jax.numpy as jnp
from jax import lax
from jax.sharding import PartitionSpec as P

D = 4096
HQ = 64
KVH = 4
HD = 128


def body(
    queries,
    keys,
    values,
    w_out,
    residual,
    norm_gain,
    expert_ids,
    gate_weights,
    w_gate,
    w_up,
    w_down,
):
    tok_rows = queries.shape[0]
    half_rows = tok_rows // 2
    exp_count = lax.axis_size("exp")
    heads_here = HQ // exp_count
    group = HQ // KVH
    kv_here = max(1, heads_here // group)
    heads_per_kv = heads_here // kv_here
    exp_index = lax.axis_index("exp")
    ctx_index = lax.axis_index("ctx")
    kv_first = exp_index * heads_here // group
    key_cols = lax.dynamic_slice_in_dim(keys, kv_first * HD, kv_here * HD, 1)
    value_cols = lax.dynamic_slice_in_dim(values, kv_first * HD, kv_here * HD, 1)
    scale = 1.0 / math.sqrt(HD)
    first_rows = queries[:half_rows]
    second_rows = queries[half_rows:]
    first_start = ctx_index * tok_rows
    second_start = ctx_index * tok_rows + half_rows
    query_sets = (
        first_rows.reshape(half_rows, kv_here, heads_per_kv, HD),
        second_rows.reshape(half_rows, kv_here, heads_per_kv, HD),
    )
    query_positions = (
        first_start + jnp.arange(half_rows, dtype=jnp.int32),
        second_start + jnp.arange(half_rows, dtype=jnp.int32),
    )
    last_positions = (first_start + half_rows - 1, second_start + half_rows - 1)

    def block_update(carry, query_four, query_pos, key_block, value_block, key_start):
        run_max, run_sum, run_acc = carry
        width = key_block.shape[0]
        key_three = key_block.reshape(width, kv_here, HD)
        value_three = value_block.reshape(width, kv_here, HD)
        scores = (
            jnp.einsum("tghd,kgd->ghtk", query_four, key_three, preferred_element_type=jnp.float32)
            * scale
        )
        key_pos = key_start + jnp.arange(width, dtype=jnp.int32)
        allowed = key_pos[None, :] <= query_pos[:, None]
        scores = jnp.where(allowed, scores, -1e30)
        new_max = jnp.maximum(run_max, jnp.max(scores, axis=-1))
        probs = jnp.where(allowed, jnp.exp(scores - new_max[..., None]), 0.0)
        factor = jnp.exp(run_max - new_max)
        run_sum = run_sum * factor + jnp.sum(probs, axis=-1)
        weighted = jnp.einsum(
            "ghtk,kgd->ghtd",
            probs.astype(jnp.bfloat16),
            value_three,
            preferred_element_type=jnp.float32,
        )
        run_acc = run_acc * factor[..., None] + weighted
        return (new_max, run_sum, run_acc)

    start_max = jnp.full((kv_here, heads_per_kv, half_rows), -1e30, jnp.float32)
    start_sum = jnp.zeros((kv_here, heads_per_kv, half_rows), jnp.float32)
    start_acc = jnp.zeros((kv_here, heads_per_kv, half_rows, HD), jnp.float32)
    start_state = (start_max, start_sum, start_acc)
    key_piece = lax.all_gather(key_cols, "ctx", axis=0, tiled=True)
    value_piece = lax.all_gather(value_cols, "ctx", axis=0, tiled=True)
    count = key_piece.shape[0]
    width = 512

    def one_block(index, inner):
        key_start = index * width
        key_block = lax.dynamic_slice_in_dim(key_piece, key_start, width, 0)
        value_block = lax.dynamic_slice_in_dim(value_piece, key_start, width, 0)
        updated = []
        for which in range(2):
            query_four = query_sets[which]
            query_pos = query_positions[which]
            updated.append(
                lax.cond(
                    key_start > last_positions[which],
                    lambda state: state,
                    lambda state: block_update(
                        state, query_four, query_pos, key_block, value_block, key_start
                    ),
                    inner[which],
                )
            )
        return (updated[0], updated[1])

    states = lax.fori_loop(0, count // width, one_block, (start_state, start_state))
    halves = []
    for which in range(2):
        run_max, run_sum, run_acc = states[which]
        halves.append(
            jnp.transpose(run_acc / run_sum[..., None], (2, 0, 1, 3))
            .reshape(half_rows, heads_here * HD)
            .astype(jnp.bfloat16)
        )
    attn_second = halves[1]
    attn = jnp.concatenate([halves[0], attn_second], axis=0)
    projected = lax.psum_scatter(
        jnp.dot(attn, w_out, preferred_element_type=jnp.float32).astype(jnp.bfloat16),
        "exp",
        scatter_dimension=0,
        tiled=True,
    ).astype(jnp.float32)
    hidden_state = (residual.astype(jnp.float32) + projected).astype(jnp.bfloat16)
    state_f = hidden_state.astype(jnp.float32)
    inv_rms = 1.0 / jnp.sqrt(jnp.mean(state_f * state_f, axis=1, keepdims=True) + 1e-06)
    normed = (state_f * inv_rms * norm_gain.astype(jnp.float32)[None, :]).astype(jnp.bfloat16)
    rows_here = expert_ids.shape[0]
    top_count = expert_ids.shape[1]
    experts_all = w_gate.shape[0] * exp_count
    capacity = min(rows_here, 2 * rows_here * top_count // experts_all)
    flat_ids = expert_ids.reshape(-1)
    onehot = (flat_ids[:, None] == jnp.arange(experts_all, dtype=jnp.int32)[None, :]).astype(
        jnp.int32
    )
    earlier = jnp.cumsum(onehot, axis=0) - onehot
    slot_index = jnp.sum(earlier * onehot, axis=1)
    target = flat_ids * capacity + slot_index
    picks = target[:, None] == jnp.arange(experts_all * capacity, dtype=jnp.int32)[None, :]
    dispatch_table = jnp.any(
        picks.reshape(rows_here, top_count, experts_all * capacity), axis=1
    ).astype(jnp.bfloat16)
    outgoing = jnp.einsum(
        "rs,rd->sd", dispatch_table, normed, preferred_element_type=jnp.float32
    ).astype(jnp.bfloat16)
    arrived = lax.all_to_all(
        outgoing.reshape(experts_all, capacity, D), "exp", split_axis=0, concat_axis=0, tiled=True
    )
    slot_rows = arrived.reshape(experts_all * capacity, D)
    gate_local = w_gate[0]
    up_local = w_up[0]
    gate_pre = jnp.dot(
        slot_rows,
        lax.all_gather(gate_local, "ctx", axis=0, tiled=True),
        preferred_element_type=jnp.float32,
    )
    up_pre = jnp.dot(
        slot_rows,
        lax.all_gather(up_local, "ctx", axis=0, tiled=True),
        preferred_element_type=jnp.float32,
    )
    expert_hidden = (jax.nn.silu(gate_pre) * up_pre).astype(jnp.bfloat16)
    down_local = w_down[0]
    expert_result = jnp.dot(
        expert_hidden,
        lax.all_gather(down_local, "ctx", axis=1, tiled=True),
        preferred_element_type=jnp.float32,
    ).astype(jnp.bfloat16)
    returned = lax.all_to_all(
        expert_result.reshape(experts_all, capacity, D),
        "exp",
        split_axis=0,
        concat_axis=0,
        tiled=True,
    )
    returned_flat = returned.reshape(experts_all * capacity, D)
    picked = jnp.dot(picks.astype(jnp.bfloat16), returned_flat, preferred_element_type=jnp.float32)
    weighted = gate_weights[:, :, None] * picked.reshape(rows_here, top_count, D)
    return (state_f + jnp.sum(weighted, axis=1)).astype(jnp.bfloat16)


def solution(mesh):
    placed = (
        P("ctx", "exp"),
        P("ctx", None),
        P("ctx", None),
        P("exp", None),
        P(("ctx", "exp"), None),
        P(),
        P(("ctx", "exp"), None),
        P(("ctx", "exp"), None),
        P("exp", "ctx", None),
        P("exp", "ctx", None),
        P("exp", None, "ctx"),
    )
    return jax.shard_map(
        body, mesh=mesh, in_specs=placed, out_specs=P(("ctx", "exp"), None), check_vma=False
    )
```

profile of v0, /device:TPU:2, one launch (start us, length us, event | category | flops | bytes accessed | tf_op | source)
XLA Modules:
  0.0 573.4 jit_solution(10112256670926563452)
XLA Ops:
  8.2 1.5 constant_dynamic-slice_fusion.3
  9.7 1.1 fusion.83
  11.5 64.9 %all-gather.11.cloned.1.call-done = bf16[8192,128]{1,0:T(8,128)(2,1)} async-done(((bf16[256,128]{1,0:T(8,128)(2,1)}), bf16[8192,128]{1,0:T(8,128)(2,1)}) %all-gather.11.cloned.1.call-update) | async-done | bytes 2097168 | tf_op jit(solution)/shard_map/all_gather | solution.py:83
  76.4 66.3 %all-gather.9.cloned.1.call-done = bf16[8192,128]{1,0:T(8,128)(2,1)} async-done(((bf16[256,128]{1,0:T(8,128)(2,1)}), bf16[8192,128]{1,0:T(8,128)(2,1)}) %all-gather.9.cloned.1.call-update) | async-done | bytes 2097168 | tf_op jit(solution)/shard_map/all_gather | solution.py:82
  142.8 54.4 %while.24 = (s32[]{:T(128)}, f32[1,8,128]{2,1,0:T(8,128)S(1)}, f32[1,8,128]{2,1,0:T(8,128)S(1)}, f32[1,8,128,128]{3,2,1,0:T(8,128)S(1)}, f32[1,8,128]{2,1,0:T(8,...) while((s32[]{:T(128)}, f32[1,8,128]{2,1,0:T(8,128)S(1)}, ...), condition=%wide.region_9.10_spmd.clone, body=%wide.region_0.9_spmd.clone.sunk | while | flops 551165184 | bytes 16921084 | solution.py:107
  142.8 1.0 constant_dynamic-slice_fusion.5
  143.8 2.0 conditional.7
  145.9 2.0 conditional.6
  148.0 1.0 constant_dynamic-slice_fusion.5
  149.0 2.0 conditional.7
  151.1 2.0 conditional.6
  153.1 1.0 constant_dynamic-slice_fusion.5
  154.1 2.0 conditional.7
  156.2 2.0 conditional.6
  158.3 1.0 constant_dynamic-slice_fusion.5
  159.3 2.0 conditional.7
  161.4 2.0 conditional.6
  163.4 1.0 constant_dynamic-slice_fusion.5
  164.5 2.0 conditional.7
  166.5 2.0 conditional.6
  168.6 1.0 constant_dynamic-slice_fusion.5
  169.6 2.0 conditional.7
  171.7 2.0 conditional.6
  173.8 1.0 constant_dynamic-slice_fusion.5
  174.8 2.0 conditional.7
  176.8 2.0 conditional.6
  178.9 1.0 constant_dynamic-slice_fusion.5
  179.9 2.0 conditional.7
  182.0 2.0 conditional.6
  184.1 1.0 constant_dynamic-slice_fusion.5
  185.1 2.0 conditional.7
  187.1 2.0 conditional.6
  189.2 1.0 constant_dynamic-slice_fusion.5
  190.4 1.0 constant_dynamic-slice_fusion.5
  191.5 1.0 constant_dynamic-slice_fusion.5
  192.7 1.0 constant_dynamic-slice_fusion.5
  195.0 1.0 constant_dynamic-slice_fusion.5
  197.8 7.1 %convolution_convert_fusion = bf16[256,4096]{1,0:T(8,128)(2,1)} fusion(bf16[1024,4096]{1,0:T(8,128)(2,1)} %param.20, bf16[128,1024]{0,1:T(8,128)(2,1)S(1)} %bitcast.139, bf16[128,1024]{0,1:T(8,128)(2,1)S(1)} %bitcast.138), kind=kOutput, calls=%fused_computation.64 | convolution fusion | flops 2149580800 | bytes 11010048 | tf_op jit(solution)/shard_map/dot_general | solution.py:119
  207.5 101.7 %reduce-scatter.2.cloned.1.call-done = bf16[32,4096]{1,0:T(8,128)(2,1)} async-done(((bf16[256,4096]{1,0:T(8,128)(2,1)}), bf16[32,4096]{1,0:T(8,128)(2,1)}) %reduce-scatter.2.cloned.1.call-update) | async-done | bytes 262160 | tf_op jit(solution)/shard_map/reduce_scatter | solution.py:118
  309.2 1.1 fusion.60
  310.3 1.5 convolution_convert_fusion.1
  311.8 25.3 %all_to_all.10 = bf16[8,16,4096]{2,1,0:T(8,128)(2,1)S(1)} all-to-all(bf16[8,16,4096]{2,1,0:T(8,128)(2,1)S(1)} %bitcast.130), channel_id=1, replica_groups=mesh['ctx'=32,'exp'=8] {'exp'}, dimensions={0} | all-to-all | bytes 2097152 | tf_op jit(solution)/shard_map/all_to_all | solution.py:146
  337.1 43.7 %all-gather.13.cloned.1.call-done = bf16[1,4096,768]{2,1,0:T(8,128)(2,1)} async-done(((bf16[1,128,768]{2,1,0:T(8,128)(2,1)}), bf16[1,4096,768]{2,1,0:T(8,128)(2,1)}) %all-gather.13.cloned.1.call-update) | async-done | bytes 6291472 | tf_op jit(solution)/shard_map/all_gather | solution.py:154
  380.8 3.8 fusion.46
  384.6 67.9 %all-gather.15.cloned.1.call-done = bf16[1,4096,768]{2,1,0:T(8,128)(2,1)} async-done(((bf16[1,128,768]{2,1,0:T(8,128)(2,1)}), bf16[1,4096,768]{2,1,0:T(8,128)(2,1)}) %all-gather.15.cloned.1.call-update) | async-done | bytes 6291472 | tf_op jit(solution)/shard_map/all_gather | solution.py:159
  452.5 82.3 %all-gather.17.cloned.1.call-done = bf16[1,768,4096]{2,1,0:T(8,128)(2,1)} async-done(((bf16[1,768,128]{2,1,0:T(8,128)(2,1)}), bf16[1,768,4096]{2,1,0:T(8,128)(2,1)}) %all-gather.17.cloned.1.call-update) | async-done | bytes 6291472 | tf_op jit(solution)/shard_map/all_gather | solution.py:166
  534.7 7.1 %fusion.48 = bf16[128,4096]{1,0:T(8,128)(2,1)S(1)} fusion(bf16[1,768,4096]{2,1,0:T(8,128)(2,1)} %all-gather.17.cloned.1.call-done, bf16[128,4096]{1,0:T(8,128)(2,1)S(1)} %bitcast.128, bf16[1,4096,768]{2,1,0:T(8,128)(2,1)} %all-gather.15.cloned.1.call-done, f32[128,768]{1,0:T(8,128)S(1)} %fusion.46), kind=kOutput, calls=%fused_computation.65 | convolution fusion | flops 1611726848 | bytes 15073280 | tf_op jit(solution)/shard_map/dot_general | solution.py:164
  541.8 23.5 %all_to_all.11 = bf16[8,16,4096]{2,1,0:T(8,128)(2,1)S(1)} all-to-all(bf16[8,16,4096]{2,1,0:T(8,128)(2,1)S(1)} %bitcast.129), channel_id=1, replica_groups=mesh['ctx'=32,'exp'=8] {'exp'}, dimensions={0} | all-to-all | bytes 2097152 | tf_op jit(solution)/shard_map/all_to_all | solution.py:169
  (290 shorter events, 44.6 us)
Async XLA Ops:
  6.5 1.0 copy-start
  6.5 69.9 %all-gather.11.cloned.1.call-start = ((), (), s32[]{:S(2)}) async-start(), calls=%async_computation.4 | async-start | bytes 2162688 | tf_op jit(solution)/shard_map/all_gather | solution.py:83
  8.1 134.5 %all-gather.9.cloned.1.call-start = ((), (), s32[]{:S(2)}) async-start(), calls=%async_computation.3 | async-start | bytes 2162688 | tf_op jit(solution)/shard_map/all_gather | solution.py:82
  9.7 299.5 %reduce-scatter.2.cloned.1.call-start = ((), (), s32[]{:S(2)}) async-start(), calls=%async_computation.5 | async-start | bytes 2359296 | tf_op jit(solution)/shard_map/reduce_scatter | solution.py:118
  204.8 1.8 copy-start.4
  204.8 2.5 copy-start.3
  204.8 104.3 %copy-start.1 = (bf16[32,4096]{1,0:T(8,128)(2,1)S(1)}, bf16[32,4096]{1,0:T(8,128)(2,1)}, u32[]{:S(2)}) copy-start(bf16[32,4096]{1,0:T(8,128)(2,1)} %param.21) | copy-start | bytes 786436
  204.9 176.0 %all-gather.13.cloned.1.call-start = ((), (), s32[]{:S(2)}) async-start(), calls=%async_computation.6 | async-start | bytes 6488064 | tf_op jit(solution)/shard_map/all_gather | solution.py:154
  205.4 247.0 %all-gather.15.cloned.1.call-start = ((), (), s32[]{:S(2)}) async-start(), calls=%async_computation.7 | async-start | bytes 6488064 | tf_op jit(solution)/shard_map/all_gather | solution.py:159
  206.0 328.7 %all-gather.17.cloned.1.call-start = ((), (), s32[]{:S(2)}) async-start(), calls=%async_computation.8 | async-start | bytes 6488064 | tf_op jit(solution)/shard_map/all_gather | solution.py:166
  541.8 23.6 %copy-start.5 = (f32[32,2]{0,1:T(2,128)S(1)}, f32[32,2]{0,1:T(2,128)}, u32[]{:S(2)}) copy-start(f32[32,2]{0,1:T(2,128)} %param.24) | copy-start | bytes 772
  541.8 23.9 %copy-start.2 = (bf16[32,4096]{1,0:T(8,128)(2,1)S(1)}, bf16[32,4096]{1,0:T(8,128)(2,1)}, u32[]{:S(2)}) copy-start(bf16[32,4096]{1,0:T(8,128)(2,1)} %reduce-scatter.2.cloned.1.call-done) | copy-start | bytes 786436
Sparse Core Ops, SparseCore 0:
  9.2 67.1 all-gather.10
  78.3 64.3 all-gather.8
  205.0 104.1 reduce-scatter.1
  310.9 69.8 all-gather.12
  382.5 69.9 all-gather.14
  454.1 80.5 all-gather.16
where the time goes:
time: 574 us; the launch traced here: 573 us
  waiting for transfers between devices  428 us (75%)
  blocking collectives  48.9 us (9%)
  matrix products  42.9 us (7%)
  local copies, waits for them, and re-layouts  21.8 us (4%)
  other arithmetic  14.7 us (3%)
  between operations  13.7 us (2%)
    reduce_scatter x1, waiting for transfers between devices, body(): lax.psum_scatter(jnp.dot(attn, w_out, preferred_element_type=jnp.float32)...  102 us
    all_gather x1, waiting for transfers between devices, body(): lax.all_gather(down_local, 'ctx', axis=1, tiled=True)  82.3 us
    all_gather x1, waiting for transfers between devices, body(): lax.all_gather(up_local, 'ctx', axis=0, tiled=True)  67.9 us
    all_gather x1, waiting for transfers between devices, body(): key_piece = lax.all_gather(key_cols, 'ctx', axis=0, tiled=True)  66.3 us
    all_gather x1, waiting for transfers between devices, body(): value_piece = lax.all_gather(value_cols, 'ctx', axis=0, tiled=True)  64.9 us
    all_gather x1, waiting for transfers between devices, body(): lax.all_gather(gate_local, 'ctx', axis=0, tiled=True)  43.7 us
    all_to_all x1, blocking collectives, body(): lax.all_to_all(outgoing.reshape(experts_all, capacity, D), 'exp', split_a...  25.3 us
    all_to_all x1, blocking collectives, body(): lax.all_to_all(expert_result.reshape(experts_all, capacity, D), 'exp', sp...  23.5 us
  transfers between devices with their start and end apart: 6, of which 6 were waited for; matrix products, arithmetic and copies ran while one was open for 2% of the time, Pallas kernels for 0%

commit v1 on v0

--- a/solution.py
+++ b/solution.py
@@ -8,6 +8,11 @@
 HQ = 64
 KVH = 4
 HD = 128
+group_shapes = lambda row_data, vector, device_axis: jnp.split(
+    lax.all_gather(jnp.concatenate([row_data, vector], axis=1), device_axis, axis=0, tiled=True),
+    [row_data.shape[1]],
+    axis=1,
+)
 
 
 def body(
@@ -79,8 +84,7 @@
     start_sum = jnp.zeros((kv_here, heads_per_kv, half_rows), jnp.float32)
     start_acc = jnp.zeros((kv_here, heads_per_kv, half_rows, HD), jnp.float32)
     start_state = (start_max, start_sum, start_acc)
-    key_piece = lax.all_gather(key_cols, "ctx", axis=0, tiled=True)
-    value_piece = lax.all_gather(value_cols, "ctx", axis=0, tiled=True)
+    key_piece, value_piece = group_shapes(key_cols, value_cols, "ctx")
     count = key_piece.shape[0]
     width = 512
 

time: 574 us -> 527 us (0.918)
  waiting for transfers between devices: 428 us -> 391 us
  blocking collectives: 48.9 us -> 23.5 us
  local copies, waits for them, and re-layouts: 21.8 us -> 31.6 us
    all_gather x2 -> x1, waiting for transfers between devices: 131 us -> 68.4 us  [lax.all_gather(jnp.concatenate([row_data, vector], axis=1), device_axis,...]
    all_to_all x1 -> x0, blocking collectives: 25.3 us -> none  [body(): lax.all_to_all(outgoing.reshape(experts_all, capacity, D), 'exp', split_a...]
    all_gather x1, waiting for transfers between devices: 43.7 us -> 63.4 us  [body(): lax.all_gather(gate_local, 'ctx', axis=0, tiled=True)]
    cond x14 -> x50, local copies, waits for them, and re-layouts: 0.04 us -> 7.39 us
  transfers between devices with their start and end apart: 6 -> 6, of which waited for: 6 -> 5; matrix products, arithmetic and copies ran while one was open for 2% -> 2% of each run, Pallas kernels for 0% -> 0%
where the time goes in v1:
time: 527 us; the launch traced here: 526 us
  waiting for transfers between devices  391 us (74%)
  matrix products  43.8 us (8%)
  local copies, waits for them, and re-layouts  31.6 us (6%)
  blocking collectives  23.5 us (4%)
  other arithmetic  15.3 us (3%)
  between operations  13.3 us (3%)
    reduce_scatter x1, waiting for transfers between devices, body(): lax.psum_scatter(jnp.dot(attn, w_out, preferred_element_type=jnp.float32)...  107 us
    all_gather x1, waiting for transfers between devices, body(): lax.all_gather(down_local, 'ctx', axis=1, tiled=True)  82.3 us
    all_gather x1, waiting for transfers between devices, lax.all_gather(jnp.concatenate([row_data, vector], axis=1), device_axis,...  68.4 us
    all_gather x1, waiting for transfers between devices, body(): lax.all_gather(up_local, 'ctx', axis=0, tiled=True)  68.2 us
    all_gather x1, waiting for transfers between devices, body(): lax.all_gather(gate_local, 'ctx', axis=0, tiled=True)  63.4 us
    all_to_all x1, blocking collectives, body(): lax.all_to_all(expert_result.reshape(experts_all, capacity, D), 'exp', sp...  23.5 us
    dot_general x18, matrix products, block_update(): jnp.einsum('ghtk,kgd->ghtd', probs.astype(jnp.bfloat16), value_three, pre...  15 us
    dynamic_slice x16, local copies, waits for them, and re-layouts, one_block(): value_block = lax.dynamic_slice_in_dim(value_piece, key_start, width, 0)  14.8 us
  transfers between devices with their start and end apart: 6, of which 5 were waited for; matrix products, arithmetic and copies ran while one was open for 2% of the time, Pallas kernels for 0%

profile of v1, /device:TPU:2, one launch (start us, length us, event | category | flops | bytes accessed | tf_op | source)
XLA Modules:
  0.0 526.0 jit_solution(14693672012487523443)
XLA Ops:
  8.2 1.1 fusion.84
  10.0 68.4 %all-gather.8.cloned.1.call-done = bf16[8192,256]{1,0:T(8,128)(2,1)} async-done(((bf16[256,256]{1,0:T(8,128)(2,1)}), bf16[8192,256]{1,0:T(8,128)(2,1)}) %all-gather.8.cloned.1.call-update) | async-done | bytes 4194320 | tf_op jit(solution)/shard_map/all_gather | solution.py:12
  78.4 3.8 fusion.83
  83.1 60.4 %while.24 = (s32[]{:T(128)}, f32[1,8,128]{2,1,0:T(8,128)S(1)}, f32[1,8,128]{2,1,0:T(8,128)S(1)}, f32[1,8,128,128]{3,2,1,0:T(8,128)S(1)}, f32[1,8,128]{2,1,0:T(8,...) while((s32[]{:T(128)}, f32[1,8,128]{2,1,0:T(8,128)S(1)}, ...), condition=%wide.region_9.10_spmd.clone, body=%wide.region_0.9_spmd.clone.sunk | while | flops 551165184 | bytes 21115444 | solution.py:111
  83.2 0.9 constant_dynamic-slice_fusion.5
  84.1 2.9 conditional.7
  87.0 2.0 conditional.6
  89.0 0.9 constant_dynamic-slice_fusion.5
  90.0 2.9 conditional.7
  92.8 2.0 conditional.6
  94.9 0.9 constant_dynamic-slice_fusion.5
  95.8 2.9 conditional.7
  98.7 2.0 conditional.6
  100.8 0.9 constant_dynamic-slice_fusion.5
  101.7 2.9 conditional.7
  104.6 2.0 conditional.6
  106.6 0.9 constant_dynamic-slice_fusion.5
  107.6 2.9 conditional.7
  110.4 2.0 conditional.6
  112.5 0.9 constant_dynamic-slice_fusion.5
  113.5 2.9 conditional.7
  116.3 2.0 conditional.6
  118.4 0.9 constant_dynamic-slice_fusion.5
  119.3 2.9 conditional.7
  122.2 2.0 conditional.6
  124.2 0.9 constant_dynamic-slice_fusion.5
  125.2 2.9 conditional.7
  128.1 2.0 conditional.6
  130.1 0.9 constant_dynamic-slice_fusion.5
  131.1 2.9 conditional.7
  133.9 2.0 conditional.6
  136.0 0.9 constant_dynamic-slice_fusion.5
  137.1 0.9 constant_dynamic-slice_fusion.5
  140.3 0.9 constant_dynamic-slice_fusion.5
  141.4 0.9 constant_dynamic-slice_fusion.5
  142.5 0.9 constant_dynamic-slice_fusion.5
  143.8 1.2 copy.50
  145.1 7.1 %convolution_convert_fusion = bf16[256,4096]{1,0:T(8,128)(2,1)} fusion(bf16[1024,4096]{1,0:T(8,128)(2,1)} %param.20, bf16[128,1024]{0,1:T(8,128)(2,1)S(1)} %bitcast.138, bf16[128,1024]{0,1:T(8,128)(2,1)S(1)} %bitcast.137), kind=kOutput, calls=%fused_computation.64 | convolution fusion | flops 2149580800 | bytes 11010048 | tf_op jit(solution)/shard_map/dot_general | solution.py:123
  155.0 107.0 %reduce-scatter.2.cloned.1.call-done = bf16[32,4096]{1,0:T(8,128)(2,1)} async-done(((bf16[256,4096]{1,0:T(8,128)(2,1)}), bf16[32,4096]{1,0:T(8,128)(2,1)}) %reduce-scatter.2.cloned.1.call-update) | async-done | bytes 262160 | tf_op jit(solution)/shard_map/reduce_scatter | solution.py:122
  262.0 1.1 fusion.60
  263.1 2.4 convolution_convert_fusion.1
  265.5 4.5 all-to-all-start
  270.1 63.4 %all-gather.10.cloned.1.call-done = bf16[1,4096,768]{2,1,0:T(8,128)(2,1)} async-done(((bf16[1,128,768]{2,1,0:T(8,128)(2,1)}), bf16[1,4096,768]{2,1,0:T(8,128)(2,1)}) %all-gather.10.cloned.1.call-update) | async-done | bytes 6291472 | tf_op jit(solution)/shard_map/all_gather | solution.py:158
  333.5 3.8 fusion.46
  337.2 68.2 %all-gather.12.cloned.1.call-done = bf16[1,4096,768]{2,1,0:T(8,128)(2,1)} async-done(((bf16[1,128,768]{2,1,0:T(8,128)(2,1)}), bf16[1,4096,768]{2,1,0:T(8,128)(2,1)}) %all-gather.12.cloned.1.call-update) | async-done | bytes 6291472 | tf_op jit(solution)/shard_map/all_gather | solution.py:163
  405.4 82.3 %all-gather.14.cloned.1.call-done = bf16[1,768,4096]{2,1,0:T(8,128)(2,1)} async-done(((bf16[1,768,128]{2,1,0:T(8,128)(2,1)}), bf16[1,768,4096]{2,1,0:T(8,128)(2,1)}) %all-gather.14.cloned.1.call-update) | async-done | bytes 6291472 | tf_op jit(solution)/shard_map/all_gather | solution.py:170
  487.7 7.1 %fusion.48 = bf16[128,4096]{1,0:T(8,128)(2,1)S(1)} fusion(bf16[1,768,4096]{2,1,0:T(8,128)(2,1)} %all-gather.14.cloned.1.call-done, bf16[128,4096]{1,0:T(8,128)(2,1)S(1)} %bitcast.128, bf16[1,4096,768]{2,1,0:T(8,128)(2,1)} %all-gather.12.cloned.1.call-done, f32[128,768]{1,0:T(8,128)S(1)} %fusion.46), kind=kOutput, calls=%fused_computation.65 | convolution fusion | flops 1611726848 | bytes 15073280 | tf_op jit(solution)/shard_map/dot_general | solution.py:168
  494.7 23.5 %all_to_all.10 = bf16[8,16,4096]{2,1,0:T(8,128)(2,1)S(1)} all-to-all(bf16[8,16,4096]{2,1,0:T(8,128)(2,1)S(1)} %bitcast.129), channel_id=1, replica_groups=mesh['ctx'=32,'exp'=8] {'exp'}, dimensions={0} | all-to-all | bytes 2097152 | tf_op jit(solution)/shard_map/all_to_all | solution.py:173
  (323 shorter events, 52.5 us)
Async XLA Ops:
  6.5 71.9 %all-gather.8.cloned.1.call-start = ((), (), s32[]{:S(2)}) async-start(), calls=%async_computation.3 | async-start | bytes 4325376 | tf_op jit(solution)/shard_map/all_gather | solution.py:12
  8.1 253.8 %reduce-scatter.2.cloned.1.call-start = ((), (), s32[]{:S(2)}) async-start(), calls=%async_computation.4 | async-start | bytes 2359296 | tf_op jit(solution)/shard_map/reduce_scatter | solution.py:122
  84.3 1.0 copy-start.2
  86.2 0.8 copy-start.3
  90.1 1.0 copy-start.2
  92.0 0.8 copy-start.3
  96.0 1.0 copy-start.2
  97.9 0.8 copy-start.3
  101.9 1.0 copy-start.2
  103.8 0.8 copy-start.3
  107.8 1.0 copy-start.2
  109.6 0.8 copy-start.3
  113.6 1.0 copy-start.2
  115.5 0.8 copy-start.3
  119.5 1.0 copy-start.2
  121.4 0.8 copy-start.3
  125.4 1.0 copy-start.2
  127.3 0.8 copy-start.3
  131.2 1.0 copy-start.2
  133.1 0.8 copy-start.3
  152.2 1.9 copy-start.5
  152.2 2.7 copy-start.4
  152.2 109.7 %copy-start = (bf16[32,4096]{1,0:T(8,128)(2,1)S(1)}, bf16[32,4096]{1,0:T(8,128)(2,1)}, u32[]{:S(2)}) copy-start(bf16[32,4096]{1,0:T(8,128)(2,1)} %param.21) | copy-start | bytes 786436
  152.2 181.2 %all-gather.10.cloned.1.call-start = ((), (), s32[]{:S(2)}) async-start(), calls=%async_computation.5 | async-start | bytes 6488064 | tf_op jit(solution)/shard_map/all_gather | solution.py:158
  153.0 252.4 %all-gather.12.cloned.1.call-start = ((), (), s32[]{:S(2)}) async-start(), calls=%async_computation.6 | async-start | bytes 6488064 | tf_op jit(solution)/shard_map/all_gather | solution.py:163
  153.6 334.1 %all-gather.14.cloned.1.call-start = ((), (), s32[]{:S(2)}) async-start(), calls=%async_computation.7 | async-start | bytes 6488064 | tf_op jit(solution)/shard_map/all_gather | solution.py:170
  265.5 67.9 %all-to-all-start = ((bf16[8,16,4096]{2,1,0:T(8,128)(2,1)}), bf16[8,16,4096]{2,1,0:T(8,128)(2,1)S(1)}, u32[]{:S(2)}, u32[]{:S(2)}) async-start(bf16[8,16,4096]{2,1,0:T(8,128)(2,1)} %bitcast.31), calls=%async_computation.1 | async-start | bytes 2097152 | tf_op jit(solution)/shard_map/all_to_all | solution.py:150
  494.7 23.6 %copy-start.6 = (f32[32,2]{0,1:T(2,128)S(1)}, f32[32,2]{0,1:T(2,128)}, u32[]{:S(2)}) copy-start(f32[32,2]{0,1:T(2,128)} %param.24) | copy-start | bytes 772
  494.7 23.9 %copy-start.1 = (bf16[32,4096]{1,0:T(8,128)(2,1)S(1)}, bf16[32,4096]{1,0:T(8,128)(2,1)}, u32[]{:S(2)}) copy-start(bf16[32,4096]{1,0:T(8,128)(2,1)} %reduce-scatter.2.cloned.1.call-done) | copy-start | bytes 786436
Sparse Core Ops, SparseCore 0:
  9.2 69.1 all-gather.7
  152.4 109.5 reduce-scatter.1
  263.8 69.5 all-gather.9
  335.2 70.1 all-gather.11
  407.0 80.5 all-gather.13
